TPU v7x, 32 devices: a whole 2x2x4 slice. The times are simulated.
32 devices in a mesh: layer: 4 (over x, core), grid: 8 (over z, y).
Axes of the slice: x: 2, y: 2, z: 4, core: 2. Of those that a mesh axis runs over, the one named last changes fastest.
Arguments:
- band_blocks: bfloat16 [80, 9, 128, 128], P('grid'), may hold values from -7 to 7, as said below
- retained: int32 [80, 9], P('grid'), may hold values from 0 to 1, as said below
Outputs:
- purified: bfloat16 [80, 9, 128, 128], P('grid', None, 'layer')
Inputs may be any that keep to these rules, and one draw needn't show every extreme that they name: `band_blocks`: the matrix is symmetric: block slot w of block row i equals the transpose of block slot 8 - w of block row (i + w - 4) mod 80. retained[i, w] = 1 exactly when retained[(i + w - 4) mod 80, 8 - w] = 1; the middle slot w = 4 is 1 in every block row.
All inputs are finite; a program needn't handle non-finite values.
Results may differ from a plain program's by a relative error of at most 0.005.
Values may be sent and summed in bfloat16 or wider, within the bound.
A program may use at most 64 MiB of HBM per device.

v0:
```python
import jax
import jax.numpy as jnp
from jax import lax
from jax.sharding import PartitionSpec as P

STEPS = 2


def extended(block, sides, width):
    for axis, dim in sides:
        count = lax.axis_size(axis)
        forward = [(i, i + 1) for i in range(count - 1)]
        forward.append((count - 1, 0))
        backward = [(target, source) for source, target in forward]
        low = lax.ppermute(
            lax.slice_in_dim(block, block.shape[dim] - width, None, axis=dim), axis, forward
        )
        high = lax.ppermute(lax.slice_in_dim(block, 0, width, axis=dim), axis, backward)
        block = jnp.concatenate([low, block, high], axis=dim)
    return block


def strip_product(left_rows, halo_rows, reach):
    row_count = left_rows.shape[0]
    band_width = left_rows.shape[1]
    padded = jnp.pad(halo_rows, ((0, 0), (reach, reach), (0, 0), (0, 0)))
    running = jnp.zeros(
        (row_count, band_width, left_rows.shape[2], halo_rows.shape[3]), jnp.float32
    )
    for offset in range(band_width):
        source = padded[
            offset : offset + row_count, 2 * reach - offset : 2 * reach - offset + band_width
        ]
        running = running + jnp.einsum(
            "rab,rwbc->rwac", left_rows[:, offset], source, preferred_element_type=jnp.float32
        )
    return running


def per_device(band_blocks, retained):
    layer_count = lax.axis_size("layer")
    share = lax.axis_index("layer")
    band_width = band_blocks.shape[1]
    block_width = band_blocks.shape[2]
    reach = (band_width - 1) // 2
    piece = block_width // layer_count
    kept = (retained != 0)[:, :, None, None]
    whole_rows = jnp.where(kept, band_blocks, jnp.zeros_like(band_blocks))
    quarter = lax.dynamic_slice_in_dim(whole_rows, share * piece, piece, 2)
    for repeat in range(STEPS):
        halo_part = extended(quarter, (("grid", 0),), reach)
        halo_rows = lax.all_gather(halo_part, "layer", axis=2, tiled=True)
        square = jnp.where(kept, strip_product(quarter, halo_rows, reach), 0.0).astype(jnp.bfloat16)
        cube = jnp.where(kept, strip_product(square, halo_rows, reach), 0.0)
        quarter = (
            (3.0 * quarter.astype(jnp.float32) - cube / (4.0 * band_width * block_width)) * 0.5
        ).astype(jnp.bfloat16)
    return quarter


def solution(mesh):
    return jax.shard_map(
        per_device,
        mesh=mesh,
        in_specs=(P("grid", None, None, None), P("grid", None)),
        out_specs=P("grid", None, "layer", None),
        check_vma=False,
    )
```

profile of v0, /device:TPU:0, one launch (start us, length us, event | category | flops | bytes accessed | tf_op | source)
XLA Modules:
  0.0 161.0 jit_solution(15024510150904314228)
XLA Ops:
  6.5 0.9 broadcast_compare_fusion
  7.5 0.9 copy-done
  8.7 3.0 %collective-permute-start = (bf16[4,9,32,128]{3,2,0,1:T(8,128)(2,1)S(1)}, bf16[4,9,32,128]{3,2,0,1:T(8,128)(2,1)S(1)}, u32[]{:S(2)}, u32[]{:S(2)}) collective-permute-start(bf16[4,9,32,128]{3,2,0,1:T(8,128)(2,1)S(1)} %get-tuple-element.7), channel_id=1, source_target_pairs={{0,1},{1,2},{2,3},{3,4},{4,5},{5,6},{6,7},{7,0},{8,9},{9,10},{10,1... | collective-permute-start | bytes 884744 | tf_op jit(solution)/shard_map/ppermute | solution.py:15
  11.7 3.1 %collective-permute-start.1 = (bf16[4,9,32,128]{3,2,0,1:T(8,128)(2,1)S(1)}, bf16[4,9,32,128]{3,2,0,1:T(8,128)(2,1)S(1)}, u32[]{:S(2)}, u32[]{:S(2)}) collective-permute-start(bf16[4,9,32,128]{3,2,0,1:T(8,128)(2,1)S(1)} %get-tuple-element.8), channel_id=1, source_target_pairs={{1,0},{2,1},{3,2},{4,3},{5,4},{6,5},{7,6},{0,7},{9,8},{10,9},{11,1... | collective-permute-start | bytes 884744 | tf_op jit(solution)/shard_map/ppermute | solution.py:18
  14.8 9.5 %collective-permute-done = bf16[4,9,32,128]{3,2,0,1:T(8,128)(2,1)S(1)} collective-permute-done((bf16[4,9,32,128]{3,2,0,1:T(8,128)(2,1)S(1)}, bf16[4,9,32,128]{3,2,0,1:T(8,128)(2,1)S(1)}, u32[]{:S(2)}, u32[]{:S(2)}) %collective-permute-start) | collective-permute-done | bytes 294944 | tf_op jit(solution)/shard_map/ppermute | solution.py:15
  24.3 2.2 %collective-permute-done.1 = bf16[4,9,32,128]{3,2,0,1:T(8,128)(2,1)S(1)} collective-permute-done((bf16[4,9,32,128]{3,2,0,1:T(8,128)(2,1)S(1)}, bf16[4,9,32,128]{3,2,0,1:T(8,128)(2,1)S(1)}, u32[]{:S(2)}, u32[]{:S(2)}) %collective-permute-start.1) | collective-permute-done | bytes 294944 | tf_op jit(solution)/shard_map/ppermute | solution.py:18
  26.5 1.3 pad_maximum_fusion
  27.8 40.9 %all-gather.3.cloned.1.call-done = bf16[18,9,128,128]{3,2,0,1:T(8,128)(2,1)} async-done(((bf16[18,9,32,128]{3,2,0,1:T(8,128)(2,1)}), bf16[18,9,128,128]{3,2,0,1:T(8,128)(2,1)}) %all-gather.3.cloned.1.call-update) | async-done | bytes 5308432 | tf_op jit(solution)/shard_map/all_gather | solution.py:52
  68.7 2.2 %fusion.24 = f32[10,9,128,32]{2,3,0,1:T(8,128)S(1)} fusion(bf16[18,9,128,128]{3,2,0,1:T(8,128)(2,1)} %all-gather.3.cloned.1.call-done, bf16[10,9,32,128]{3,2,0,1:T(8,128)(2,1)} %copy-done.7), kind=kOutput, calls=%fused_computation.44 | convolution fusion | flops 94371840 | bytes 6864896 | tf_op jit(solution)/shard_map/rab,rwbc->rwac/dot_general | solution.py:34
  71.0 0.9 copy-done.2
  72.5 0.6 fusion.20
  73.1 0.6 fusion.18
  73.7 0.5 fusion.16
  74.6 0.5 fusion.12
  75.1 0.6 fusion.4
  75.7 0.9 fusion.40
  76.6 0.5 fusion.25
  77.0 0.5 fusion.23
  77.5 0.6 fusion.21
  78.1 0.6 fusion.6
  78.7 0.6 fusion.19
  79.2 0.5 fusion.17
  80.2 0.5 fusion.13
  80.7 1.1 fusion.11
  81.9 1.5 collective-permute-start.2
  83.4 3.3 %collective-permute-start.3 = (bf16[4,9,32,128]{3,2,0,1:T(8,128)(2,1)S(1)}, bf16[4,9,32,128]{3,2,0,1:T(8,128)(2,1)S(1)}, u32[]{:S(2)}, u32[]{:S(2)}) collective-permute-start(bf16[4,9,32,128]{3,2,0,1:T(8,128)(2,1)S(1)} %get-tuple-element.6), channel_id=1, source_target_pairs={{1,0},{2,1},{3,2},{4,3},{5,4},{6,5},{7,6},{0,7},{9,8},{10,9},{11,1... | collective-permute-start | bytes 884744 | tf_op jit(solution)/shard_map/ppermute | solution.py:18
  86.7 9.8 %collective-permute-done.2 = bf16[4,9,32,128]{3,2,0,1:T(8,128)(2,1)S(1)} collective-permute-done((bf16[4,9,32,128]{3,2,0,1:T(8,128)(2,1)S(1)}, bf16[4,9,32,128]{3,2,0,1:T(8,128)(2,1)S(1)}, u32[]{:S(2)}, u32[]{:S(2)}) %collective-permute-start.2) | collective-permute-done | bytes 294944 | tf_op jit(solution)/shard_map/ppermute | solution.py:15
  96.4 2.2 %collective-permute-done.3 = bf16[4,9,32,128]{3,2,0,1:T(8,128)(2,1)S(1)} collective-permute-done((bf16[4,9,32,128]{3,2,0,1:T(8,128)(2,1)S(1)}, bf16[4,9,32,128]{3,2,0,1:T(8,128)(2,1)S(1)}, u32[]{:S(2)}, u32[]{:S(2)}) %collective-permute-start.3) | collective-permute-done | bytes 294944 | tf_op jit(solution)/shard_map/ppermute | solution.py:18
  98.6 1.3 pad_maximum_fusion.1
  99.9 39.7 %all-gather.5.cloned.1.call-done = bf16[18,9,128,128]{3,2,0,1:T(8,128)(2,1)} async-done(((bf16[18,9,32,128]{3,2,0,1:T(8,128)(2,1)}), bf16[18,9,128,128]{3,2,0,1:T(8,128)(2,1)}) %all-gather.5.cloned.1.call-update) | async-done | bytes 5308432 | tf_op jit(solution)/shard_map/all_gather | solution.py:52
  139.7 2.2 %fusion.38 = f32[10,9,128,32]{2,3,0,1:T(8,128)S(1)} fusion(bf16[18,9,128,128]{3,2,0,1:T(8,128)(2,1)} %all-gather.5.cloned.1.call-done, bf16[10,9,32,128]{3,2,0,1:T(8,128)(2,1)} %copy-done.4), kind=kOutput, calls=%fused_computation.58 | convolution fusion | flops 94371840 | bytes 6864896 | tf_op jit(solution)/shard_map/rab,rwbc->rwac/dot_general | solution.py:34
  141.9 0.9 copy-done.3
  142.8 0.5 fusion.36
  143.3 0.6 fusion.34
  143.8 0.6 fusion.32
  144.4 0.5 fusion.30
  145.4 0.5 fusion.26
  145.9 0.6 fusion
  146.4 1.0 fusion.41
  147.9 0.5 fusion.37
  148.4 0.6 fusion.35
  149.0 0.6 fusion.2
  149.5 0.6 fusion.33
  150.1 0.5 fusion.31
  151.1 0.5 fusion.27
  151.6 0.6 copy-done.6
  152.2 1.0 fusion.9
  153.2 0.9 copy.78
  (28 shorter events, 3.5 us)
Async XLA Ops:
  6.5 1.8 %copy-start = (bf16[10,9,128,128]{3,2,1,0:T(8,128)(2,1)S(1)}, bf16[10,9,128,128]{3,2,1,0:T(8,128)(2,1)}, u32[]{:S(2)}) copy-start(bf16[10,9,128,128]{3,2,1,0:T(8,128)(2,1)} %param.2) | copy-start | bytes 8847364
  6.5 62.2 %all-gather.3.cloned.1.call-start = ((), (), s32[]{:S(2)}) async-start(), calls=%async_computation | async-start | bytes 6635520 | tf_op jit(solution)/shard_map/all_gather | solution.py:52
  8.6 17.9 %copy-start.7 = (bf16[10,9,32,128]{3,2,0,1:T(8,128)(2,1)}, bf16[10,9,32,128]{3,2,0,1:T(8,128)(2,1)S(1)}, u32[]{:S(2)}) copy-start(bf16[10,9,32,128]{3,2,0,1:T(8,128)(2,1)S(1)} %copy_select_fusion) | copy-start | bytes 2211844
  8.7 15.6 %collective-permute-start = (bf16[4,9,32,128]{3,2,0,1:T(8,128)(2,1)S(1)}, bf16[4,9,32,128]{3,2,0,1:T(8,128)(2,1)S(1)}, u32[]{:S(2)}, u32[]{:S(2)}) collective-permute-start(bf16[4,9,32,128]{3,2,0,1:T(8,128)(2,1)S(1)} %get-tuple-element.7), channel_id=1, source_target_pairs={{0,1},{1,2},{2,3},{3,4},{4,5},{5,6},{6,7},{7,0},{8,9},{9,10},{10,1... | collective-permute-start | bytes 884744 | tf_op jit(solution)/shard_map/ppermute | solution.py:15
  11.7 14.8 %collective-permute-start.1 = (bf16[4,9,32,128]{3,2,0,1:T(8,128)(2,1)S(1)}, bf16[4,9,32,128]{3,2,0,1:T(8,128)(2,1)S(1)}, u32[]{:S(2)}, u32[]{:S(2)}) collective-permute-start(bf16[4,9,32,128]{3,2,0,1:T(8,128)(2,1)S(1)} %get-tuple-element.8), channel_id=1, source_target_pairs={{1,0},{2,1},{3,2},{4,3},{5,4},{6,5},{7,6},{0,7},{9,8},{10,9},{11,1... | collective-permute-start | bytes 884744 | tf_op jit(solution)/shard_map/ppermute | solution.py:18
  27.8 111.9 %all-gather.5.cloned.1.call-start = ((), (), s32[]{:S(2)}) async-start(), calls=%async_computation.1 | async-start | bytes 6635520 | tf_op jit(solution)/shard_map/all_gather | solution.py:52
  68.7 3.1 %copy-start.2 = (bf16[18,9,128,128]{3,2,0,1:T(8,128)(2,1)S(1)}, bf16[18,9,128,128]{3,2,0,1:T(8,128)(2,1)}, u32[]{:S(2)}) copy-start(bf16[18,9,128,128]{3,2,0,1:T(8,128)(2,1)} %all-gather.3.cloned.1.call-done) | copy-start | bytes 15925252
  68.7 3.3 %copy-start.8 = (bf16[10,9,32,128]{3,2,0,1:T(8,128)(2,1)S(1)}, bf16[10,9,32,128]{3,2,0,1:T(8,128)(2,1)}, u32[]{:S(2)}) copy-start(bf16[10,9,32,128]{3,2,0,1:T(8,128)(2,1)} %copy-done.7) | copy-start | bytes 2211844
  81.8 16.8 %copy-start.4 = (bf16[10,9,32,128]{3,2,0,1:T(8,128)(2,1)}, bf16[10,9,32,128]{3,2,0,1:T(8,128)(2,1)S(1)}, u32[]{:S(2)}) copy-start(bf16[10,9,32,128]{3,2,0,1:T(8,128)(2,1)S(1)} %fusion.11) | copy-start | bytes 2211844
  81.9 14.5 %collective-permute-start.2 = (bf16[4,9,32,128]{3,2,0,1:T(8,128)(2,1)S(1)}, bf16[4,9,32,128]{3,2,0,1:T(8,128)(2,1)S(1)}, u32[]{:S(2)}, u32[]{:S(2)}) collective-permute-start(bf16[4,9,32,128]{3,2,0,1:T(8,128)(2,1)S(1)} %get-tuple-element.5), channel_id=1, source_target_pairs={{0,1},{1,2},{2,3},{3,4},{4,5},{5,6},{6,7},{7,0},{8,9},{9,10},{10,1... | collective-permute-start | bytes 884744 | tf_op jit(solution)/shard_map/ppermute | solution.py:15
  83.4 15.2 %collective-permute-start.3 = (bf16[4,9,32,128]{3,2,0,1:T(8,128)(2,1)S(1)}, bf16[4,9,32,128]{3,2,0,1:T(8,128)(2,1)S(1)}, u32[]{:S(2)}, u32[]{:S(2)}) collective-permute-start(bf16[4,9,32,128]{3,2,0,1:T(8,128)(2,1)S(1)} %get-tuple-element.6), channel_id=1, source_target_pairs={{1,0},{2,1},{3,2},{4,3},{5,4},{6,5},{7,6},{0,7},{9,8},{10,9},{11,1... | collective-permute-start | bytes 884744 | tf_op jit(solution)/shard_map/ppermute | solution.py:18
  99.9 42.0 %copy-start.5 = (bf16[10,9,32,128]{3,2,0,1:T(8,128)(2,1)S(1)}, bf16[10,9,32,128]{3,2,0,1:T(8,128)(2,1)}, u32[]{:S(2)}) copy-start(bf16[10,9,32,128]{3,2,0,1:T(8,128)(2,1)} %copy-done.4) | copy-start | bytes 2211844
  139.7 3.1 %copy-start.3 = (bf16[18,9,128,128]{3,2,0,1:T(8,128)(2,1)S(1)}, bf16[18,9,128,128]{3,2,0,1:T(8,128)(2,1)}, u32[]{:S(2)}) copy-start(bf16[18,9,128,128]{3,2,0,1:T(8,128)(2,1)} %all-gather.5.cloned.1.call-done) | copy-start | bytes 15925252
  151.1 1.1 copy-start.6
  152.2 1.9 %copy-start.1 = (bf16[10,9,128,128]{3,2,1,0:T(8,128)(2,1)S(1)}, bf16[10,9,128,128]{3,2,1,0:T(8,128)(2,1)}, u32[]{:S(2)}) copy-start(bf16[10,9,128,128]{3,2,1,0:T(8,128)(2,1)} %param.2) | copy-start | bytes 8847364
Sparse Core Ops, SparseCore 0:
  27.9 40.7 all-gather.2
  100.0 39.5 all-gather.4
where the time goes:
time: 161 us
  waiting for transfers between devices  104 us (65%)
  matrix products  23.9 us (15%)
  between operations  13.6 us (8%)
  starting transfers between devices  11 us (7%)
  local copies, waits for them, and re-layouts  4.62 us (3%)
  other arithmetic  3.59 us (2%)
    all_gather x2, waiting for transfers between devices, per_device(): halo_rows = lax.all_gather(halo_part, 'layer', axis=2, tiled=True)  80.6 us
    dot_general x36, matrix products, strip_product(): jnp.einsum('rab,rwbc->rwac', left_rows[:, offset], source, preferred_elem...  23.9 us
    ppermute x2, waiting for transfers between devices, extended(): lax.ppermute(lax.slice_in_dim(block, block.shape[dim] - width, None, axis...  19.2 us
    ppermute x2, starting transfers between devices, extended(): lax.ppermute(lax.slice_in_dim(block, 0, width, axis=dim), axis, backward)  6.36 us
    ppermute x2, starting transfers between devices, extended(): lax.ppermute(lax.slice_in_dim(block, block.shape[dim] - width, None, axis...  4.57 us
    ppermute x2, waiting for transfers between devices, extended(): lax.ppermute(lax.slice_in_dim(block, 0, width, axis=dim), axis, backward)  4.4 us
    unnamed x18, local copies, waits for them, and re-layouts  3.52 us
  transfers between devices with their start and end apart: 6, of which 6 were waited for; matrix products, arithmetic and copies ran while one was open for 0% of the time, Pallas kernels for 0%

commit v1 on v0

v1 whole, which is shorter than its diff:
```python
import functools

import jax
import jax.numpy as jnp
from jax import lax
from jax.experimental import pallas as pl
from jax.experimental.pallas import tpu as pltpu
from jax.sharding import PartitionSpec as P

MESH = pl.DeviceIdType.MESH


def exchange(dims, x_ref, r_ref, h_ref, r3_ref, send, recv, r_send, r_recv, local):
    layers, grids, rows, reach, piece = dims
    depth = 2 * reach
    q = lax.axis_index("layer")
    g = lax.axis_index("grid")
    right = lax.rem(g + 1, grids)
    left = lax.rem(g + grids - 1, grids)
    far = lax.rem(q + layers // 2, layers)
    near = q + 1 - 2 * lax.rem(q, 2)

    barrier = pltpu.get_barrier_semaphore()
    peers = ((q, left), (q, right), (far, g), (near, g))
    for peer in peers:
        pl.semaphore_signal(barrier, inc=1, device_id=peer, device_id_type=MESH)
    pl.semaphore_wait(barrier, len(peers))

    mine = pl.ds(pl.multiple_of(q * piece, piece), piece)
    fars = pl.ds(pl.multiple_of(far * piece, piece), piece)

    def copy(stage, side, j, source, target, peer):
        return pltpu.make_async_remote_copy(
            src_ref=source,
            dst_ref=target,
            send_sem=send.at[stage, side, j],
            recv_sem=recv.at[stage, side, j],
            device_id=peer,
            device_id_type=MESH,
        )

    copies = {}
    for j in range(depth):
        count = min(reach + 1, depth - j)
        for side in range(2):
            first = rows - depth if side == 0 else 0
            there = h_ref.at[side, j, 0:count, mine, :]
            beyond = h_ref.at[side, j, 0:count, fars, :]
            source = x_ref.at[first + j, reach : reach + count, mine, :]
            copies[0, side, j] = copy(
                0, side, j, source, there, (q, right if side == 0 else left)
            )
            copies[1, side, j] = copy(1, side, j, there, there, (far, g))
            copies[2, side, j] = copy(2, side, j, there, there, (near, g))
            copies[3, side, j] = copy(3, side, j, beyond, beyond, (near, g))
            copies[0, side, j].start()
    flags = []
    for side in range(2):
        flags.append(
            pltpu.make_async_remote_copy(
                src_ref=r_ref,
                dst_ref=r3_ref.at[2 * side],
                send_sem=r_send.at[side],
                recv_sem=r_recv.at[side],
                device_id=(q, right if side == 0 else left),
                device_id_type=MESH,
            )
        )
        flags[side].start()
    own = pltpu.make_async_copy(r_ref, r3_ref.at[1], local)
    own.start()
    for j in range(depth + 1):
        for side in range(2):
            if j < depth:
                copies[0, side, j].wait_recv()
                copies[1, side, j].start()
                copies[2, side, j].start()
            if j > 0:
                copies[1, side, j - 1].wait_recv()
                copies[3, side, j - 1].start()
    for j in range(depth):
        for side in range(2):
            copies[2, side, j].wait_recv()
            copies[3, side, j].wait_recv()
            for stage in range(4):
                copies[stage, side, j].wait_send()
    for flag in flags:
        flag.wait()
    own.wait()


def purify(dims, r3, x_ref, h_ref, o_ref, wide, cur, strip, part, part_square):
    rows, reach, block, piece = dims
    band = 2 * reach + 1
    depth = 2 * reach
    tile = 2 * block
    span = reach // 2
    scale = 1.0 / (4.0 * band * block)
    q = lax.axis_index("layer")
    total = rows + 2 * depth
    tiles = rows // 2
    mids = tiles + 2 * span

    def kept(r, w):
        place = r + rows
        return r3[lax.div(place, rows), lax.rem(place, rows), w] if not isinstance(place, int) else r3[
            place // rows, place % rows, w
        ]

    def masked(value, r, w):
        return jnp.where(kept(r, w) != 0, value, jnp.zeros_like(value))

    def put(r, c, value):
        wide[
            (r + depth) * block : (r + depth + 1) * block,
            (c + depth) * block : (c + depth + 1) * block,
        ] = value

    empty = jnp.zeros((block, block), jnp.bfloat16)
    for t in range(total // 2):
        r = 2 * t - depth
        if r + reach + 1 < rows + depth:
            put(r, r + reach + 1, empty)
        if r - reach >= -depth:
            put(r + 1, r - reach, empty)
    for r in range(rows):
        for w in range(band):
            c = r + w - reach
            value = masked(x_ref[r, w], r, w)
            put(r, c, value)
            if c < 0 or c >= rows:
                put(c, r, value.T)
    for side in range(2):
        for j in range(depth):
            r = j - depth if side == 0 else rows + j
            for s in range(min(reach + 1, depth - j)):
                value = masked(h_ref[side, j, s], r, reach + s)
                put(r, r + s, value)
                if s > 0:
                    put(r + s, r, value.T)

    def ranges(d):
        low = max(0, d - span)
        high = min(2 * span, d + span)
        return low, high + 1

    def step(i, carry):
        top = pl.multiple_of((i + span) * tile, tile)
        left = pl.multiple_of(i * tile, tile)
        for d in range(2 * span + 1):
            low, high = ranges(d)
            inner = pl.ds(left + low * tile, (high - low) * tile)
            columns = pl.ds(left + d * tile, tile)
            product = jnp.dot(
                wide[pl.ds(top, tile), inner],
                wide[inner, columns],
                preferred_element_type=jnp.float32,
            )
            for a in range(2):
                for b in range(2):
                    w = 2 * (d - span) + b - a + reach
                    value = product[a * block : (a + 1) * block, b * block : (b + 1) * block]
                    if 0 <= w < band:
                        value = masked(value, 2 * i - reach + a, w)
                    else:
                        value = jnp.zeros_like(value)
                    strip[
                        a * block : (a + 1) * block,
                        d * tile + b * block : d * tile + (b + 1) * block,
                    ] = value.astype(jnp.bfloat16)
        for d in range(2 * span + 1):
            low, high = ranges(d)
            inner = pl.ds(left + low * tile, (high - low) * tile)
            columns = pl.ds(left + d * tile, tile)
            product = jnp.dot(
                strip[:, low * tile : high * tile],
                wide[inner, columns],
                preferred_element_type=jnp.float32,
            )
            value = (
                3.0 * wide[pl.ds(top, tile), columns].astype(jnp.float32) - product * scale
            ) * 0.5
            for a in range(2):
                for b in range(2):
                    w = 2 * (d - span) + b - a + reach
                    piece_value = value[a * block : (a + 1) * block, b * block : (b + 1) * block]
                    if 0 <= w < band:
                        piece_value = masked(piece_value, 2 * i - reach + a, w)
                    else:
                        piece_value = jnp.zeros_like(piece_value)
                    cur[
                        pl.ds(pl.multiple_of(i * tile + a * block, block), block),
                        pl.ds(pl.multiple_of(left + d * tile + b * block, block), block),
                    ] = piece_value.astype(jnp.bfloat16)
        return carry

    lax.fori_loop(0, mids, step, 0)

    part[...] = jnp.zeros_like(part)
    part_square[...] = jnp.zeros_like(part_square)
    for r in range(rows):
        start = pl.multiple_of((r + reach) * block + q * piece, piece)
        part[r * piece : (r + 1) * piece, r * block : (r + band) * block] = cur[
            pl.ds(start, piece), (r + reach) * block : (r + reach + band) * block
        ]

    def columns_of(c, left):
        low, high = max(0, c - span), min(mids, c + span + 1)
        first, last = max(0, c - 2 * span), min(tiles, c + 1)
        product = jnp.dot(
            left[first * 2 * piece : last * 2 * piece, low * tile : high * tile],
            cur[low * tile : high * tile, (c + span) * tile : (c + span + 1) * tile],
            preferred_element_type=jnp.float32,
        )
        for r in range(2 * first, 2 * last):
            for b in range(2):
                w = 2 * c + b - r
                if 0 <= w < band:
                    at = (r - 2 * first) * piece
                    yield r, w, product[at : at + piece, b * block : (b + 1) * block]

    for c in range(mids):
        for r, w, value in columns_of(c, part):
            part_square[
                r * piece : (r + 1) * piece, (r + w) * block : (r + w + 1) * block
            ] = masked(value, r, w).astype(jnp.bfloat16)
    for c in range(mids):
        for r, w, value in columns_of(c, part_square):
            before = part[r * piece : (r + 1) * piece, (r + w) * block : (r + w + 1) * block]
            after = (3.0 * before.astype(jnp.float32) - value * scale) * 0.5
            o_ref[r, w] = masked(after, r, w).astype(jnp.bfloat16)


def per_device(layers, grids, band_blocks, retained):
    rows, band, block, _ = band_blocks.shape
    reach = (band - 1) // 2
    depth = 2 * reach
    piece = block // layers
    dtype = band_blocks.dtype
    anywhere = pl.BlockSpec(memory_space=pl.ANY)
    halo, flags = pl.pallas_call(
        functools.partial(exchange, (layers, grids, rows, reach, piece)),
        out_shape=(
            jax.ShapeDtypeStruct((2, depth, reach + 1, block, block), dtype),
            jax.ShapeDtypeStruct((3, rows, band), retained.dtype),
        ),
        in_specs=[anywhere, anywhere],
        out_specs=(anywhere, anywhere),
        scratch_shapes=[
            pltpu.SemaphoreType.DMA((4, 2, depth)),
            pltpu.SemaphoreType.DMA((4, 2, depth)),
            pltpu.SemaphoreType.DMA((2,)),
            pltpu.SemaphoreType.DMA((2,)),
            pltpu.SemaphoreType.DMA,
        ],
        compiler_params=pltpu.CompilerParams(collective_id=0, has_side_effects=True),
        name="exchange",
    )(band_blocks, retained)
    tile = 2 * block
    total = (rows + 2 * depth) * block
    middle = (rows + depth) * block
    inside = pl.BlockSpec(memory_space=pltpu.VMEM)
    return pl.pallas_call(
        functools.partial(purify, (rows, reach, block, piece)),
        out_shape=jax.ShapeDtypeStruct((rows, band, piece, block), dtype),
        in_specs=[pl.BlockSpec(memory_space=pltpu.SMEM), inside, inside],
        out_specs=inside,
        scratch_shapes=[
            pltpu.VMEM((total, total), dtype),
            pltpu.VMEM((middle, total), dtype),
            pltpu.VMEM((tile, (reach + 1) * tile), dtype),
            pltpu.VMEM((rows * piece, middle), dtype),
            pltpu.VMEM((rows * piece, middle), dtype),
        ],
        compiler_params=pltpu.CompilerParams(vmem_limit_bytes=60 * 1024 * 1024),
        name="purify",
    )(flags, band_blocks, halo)


def solution(mesh):
    return jax.shard_map(
        functools.partial(per_device, mesh.shape["layer"], mesh.shape["grid"]),
        mesh=mesh,
        in_specs=(P("grid", None, None, None), P("grid", None)),
        out_specs=P("grid", None, "layer", None),
        check_vma=False,
    )
```

time: 161 us -> 54.7 us (0.34)
  waiting for transfers between devices: 104 us -> 0 us
  Pallas kernels: 0 us -> 54.3 us
  matrix products: 23.9 us -> 0 us
  between operations: 13.6 us -> 0.01 us
  starting transfers between devices: 11 us -> 0 us
  local copies, waits for them, and re-layouts: 4.62 us -> 0 us
  other arithmetic: 3.59 us -> 0 us
    all_gather x2 -> x0, waiting for transfers between devices: 80.6 us -> none  [per_device(): halo_rows = lax.all_gather(halo_part, 'layer', axis=2, tiled=True)]
    pallas_call x0 -> x2, Pallas kernels: none -> 54.3 us  [the longest x1 32.7 us: per_device(): pl.pallas_call(functools.partial(exchange, (layers, grids, rows, reach, p...]
    dot_general x36 -> x0, matrix products: 23.9 us -> none  [strip_product(): jnp.einsum('rab,rwbc->rwac', left_rows[:, offset], source, preferred_elem...]
    ppermute x4 -> x0, waiting for transfers between devices: 23.6 us -> none  [the longest x2 19.2 us: extended(): lax.ppermute(lax.slice_in_dim(block, block.shape[dim] - width, None, axis...]
    ppermute x4 -> x0, starting transfers between devices: 10.9 us -> none  [the longest x2 6.36 us: extended(): lax.ppermute(lax.slice_in_dim(block, 0, width, axis=dim), axis, backward)]
    unnamed x18 -> x0, local copies, waits for them, and re-layouts: 3.52 us -> none
    concatenate x2 -> x0, other arithmetic: 2.51 us -> none  [extended(): block = jnp.concatenate([low, block, high], axis=dim)]
  transfers between devices with their start and end apart: 6 -> 0, of which waited for: 6 -> 0; matrix products, arithmetic and copies ran while one was open for 0% -> 0% of each run, Pallas kernels for 0% -> 0%
where the time goes in v1:
time: 54.7 us; the launch traced here: 54.4 us
  Pallas kernels  54.3 us (99%)
    pallas_call x1, Pallas kernels, per_device(): pl.pallas_call(functools.partial(exchange, (layers, grids, rows, reach, p...  32.7 us
    pallas_call x1, Pallas kernels, per_device(): pl.pallas_call(functools.partial(purify, (rows, reach, block, piece)), ou...  21.6 us

profile of v1, /device:TPU:0, one launch (start us, length us, event | category | flops | bytes accessed | tf_op | source)
XLA Modules:
  0.0 54.4 jit_solution(9779238566838260658)
XLA Ops:
  0.0 32.7 %exchange.1 = (bf16[2,8,5,128,128]{4,3,2,1,0:T(8,128)(2,1)}, s32[3,10,9]{2,1,0:T(8,128)}) custom-call(bf16[10,9,128,128]{3,2,1,0:T(8,128)(2,1)} %x_ref.3, s32[10,9]{1,0:T(8,128)} %r_ref.1), custom_call_target="tpu_custom_call" | custom-call | tf_op jit(solution)/shard_map/exchange/pallas_call | solution.py:241
  32.7 21.6 %purify.1 = bf16[10,9,32,128]{3,2,1,0:T(8,128)(2,1)} custom-call(s32[3,10,9]{2,1,0:T(8,128)} %get-tuple-element.7.r3, bf16[10,9,128,128]{3,2,1,0:T(8,128)(2,1)} %x_ref.3, bf16[2,8,5,128,128]{4,3,2,1,0:T(8,128)(2,1)} %get-tuple-element.8.h_ref), custom_call_target="tpu_custom_call" | custom-call | tf_op jit(solution)/shard_map/purify/pallas_call | solution.py:263

commit v2 on v0

v2 whole, which is shorter than its diff:
```python
import functools

import jax
import jax.numpy as jnp
from jax import lax
from jax.experimental import pallas as pl
from jax.experimental.pallas import tpu as pltpu
from jax.sharding import PartitionSpec as P

MESH = pl.DeviceIdType.MESH


def purify(dims, x_hbm, r_hbm, o_ref, x_ref, halo, flags, r3, wide, cur, strip, part, part_square,
           send, recv, r_send, r_recv, local):
    layers, grids, rows, reach, block = dims
    piece = block // layers
    band = 2 * reach + 1
    depth = 2 * reach
    tile = 2 * block
    span = reach // 2
    scale = 1.0 / (4.0 * band * block)
    total = rows + 2 * depth
    tiles = rows // 2
    mids = tiles + 2 * span
    centre = mids // 2

    q = lax.axis_index("layer")
    g = lax.axis_index("grid")
    right = lax.rem(g + 1, grids)
    left = lax.rem(g + grids - 1, grids)
    far = lax.rem(q + layers // 2, layers)
    near = q + 1 - 2 * lax.rem(q, 2)

    own_flags = pltpu.make_async_copy(r_hbm, r3.at[1], local.at[0])
    own_flags.start()
    own_blocks = pltpu.make_async_copy(x_hbm, x_ref, local.at[1])
    own_blocks.start()

    barrier = pltpu.get_barrier_semaphore()
    peers = ((q, left), (q, right), (far, g), (near, g))
    for peer in peers:
        pl.semaphore_signal(barrier, inc=1, device_id=peer, device_id_type=MESH)
    pl.semaphore_wait(barrier, len(peers))

    mine = pl.ds(pl.multiple_of(q * piece, piece), piece)
    fars = pl.ds(pl.multiple_of(far * piece, piece), piece)

    def copy(stage, side, j, source, target, peer):
        return pltpu.make_async_remote_copy(
            src_ref=source,
            dst_ref=target,
            send_sem=send.at[stage, side, j],
            recv_sem=recv.at[stage, side, j],
            device_id=peer,
            device_id_type=MESH,
        )

    sides = ((q, right), (q, left))
    copies = {}
    flag_copies = []
    for side in range(2):
        flag_copies.append(
            pltpu.make_async_remote_copy(
                src_ref=r_hbm,
                dst_ref=flags.at[side],
                send_sem=r_send.at[side],
                recv_sem=r_recv.at[side],
                device_id=sides[side],
                device_id_type=MESH,
            )
        )
    for j in range(depth):
        count = min(reach + 1, j + 1)
        for side in range(2):
            there = halo.at[side, j, 0:count, mine, :]
            beyond = halo.at[side, j, 0:count, fars, :]
            if side == 0:
                source = x_hbm.at[rows - 1 - j, reach : reach + count, mine, :]
            else:
                source = x_hbm.at[j, reach + 1 - count : reach + 1, mine, :]
            copies[0, side, j] = copy(0, side, j, source, there, sides[side])
            copies[1, side, j] = copy(1, side, j, there, there, (far, g))
            copies[2, side, j] = copy(2, side, j, there, there, (near, g))
            copies[3, side, j] = copy(3, side, j, beyond, beyond, (near, g))
            copies[0, side, j].start()
        if j == 1:
            for side in range(2):
                flag_copies[side].start()

    def forward(*js):
        for j in js:
            for side in range(2):
                copies[0, side, j].wait_recv()
                copies[1, side, j].start()
                copies[2, side, j].start()

    def share(*js):
        for j in js:
            for side in range(2):
                copies[1, side, j].wait_recv()
                copies[3, side, j].start()

    def masked(value, r, w):
        place = r + rows
        return jnp.where(r3[place // rows, place % rows, w] != 0, value, jnp.zeros_like(value))

    def put(r, c, value):
        wide[
            (r + depth) * block : (r + depth + 1) * block,
            (c + depth) * block : (c + depth + 1) * block,
        ] = value

    def build(*js):
        for j in js:
            for side in range(2):
                copies[2, side, j].wait_recv()
                copies[3, side, j].wait_recv()
                count = min(reach + 1, j + 1)
                r = -1 - j if side == 0 else rows + j
                for s in range(count):
                    w = reach + s if side == 0 else reach + 1 - count + s
                    c = r + w - reach
                    value = masked(halo[side, j, s], r, w)
                    put(r, c, value)
                    if c != r:
                        put(c, r, value.T)

    def ranges(d):
        low = max(0, d - span)
        high = min(2 * span, d + span)
        return low, high + 1

    def step(i):
        rows_at = slice((i + span) * tile, (i + span + 1) * tile)
        for d in range(2 * span + 1):
            low, high = ranges(d)
            inner = slice((i + low) * tile, (i + high) * tile)
            columns = slice((i + d) * tile, (i + d + 1) * tile)
            product = jnp.dot(
                wide[rows_at, inner], wide[inner, columns], preferred_element_type=jnp.float32
            )
            for a in range(2):
                for b in range(2):
                    w = 2 * (d - span) + b - a + reach
                    if 0 <= w < band:
                        value = masked(
                            product[a * block : (a + 1) * block, b * block : (b + 1) * block],
                            2 * i - reach + a,
                            w,
                        ).astype(jnp.bfloat16)
                    else:
                        value = jnp.zeros((block, block), jnp.bfloat16)
                    at = d * tile + b * block
                    strip[a * block : (a + 1) * block, at : at + block] = value
        for d in range(2 * span + 1):
            if not 0 <= i + d - span < mids:
                continue
            low, high = ranges(d)
            inner = slice((i + low) * tile, (i + high) * tile)
            columns = slice((i + d) * tile, (i + d + 1) * tile)
            product = jnp.dot(
                strip[:, low * tile : high * tile],
                wide[inner, columns],
                preferred_element_type=jnp.float32,
            )
            value = (3.0 * wide[rows_at, columns].astype(jnp.float32) - product * scale) * 0.5
            for a in range(2):
                for b in range(2):
                    w = 2 * (d - span) + b - a + reach
                    if 0 <= w < band:
                        result = masked(
                            value[a * block : (a + 1) * block, b * block : (b + 1) * block],
                            2 * i - reach + a,
                            w,
                        ).astype(jnp.bfloat16)
                    else:
                        result = jnp.zeros((block, block), jnp.bfloat16)
                    down = i * tile + a * block
                    at = (i + d - span) * tile + b * block
                    cur[down : down + block, at : at + block] = result

    empty = jnp.zeros((block, block), jnp.bfloat16)
    for t in range(total // 2):
        r = 2 * t - depth
        if r + reach + 1 < rows + depth:
            put(r, r + reach + 1, empty)
        if r - reach >= -depth:
            put(r + 1, r - reach, empty)
    own_flags.wait()
    own_blocks.wait()
    for r in range(rows):
        for w in range(band):
            c = r + w - reach
            value = masked(x_ref[r, w], r, w)
            put(r, c, value)
            if c < 0 or c >= rows:
                put(c, r, value.T)

    forward(*range(reach))
    step(centre)
    for side in range(2):
        flag_copies[side].wait_recv()
        landed = pltpu.make_async_copy(flags.at[side], r3.at[2 * side], local.at[0])
        landed.start()
        landed.wait()
    forward(reach)
    share(0, 1)
    forward(reach + 1)
    sent = 2
    for near_by in range(1, span + tiles // 2 + 1):
        build(*range(2 * near_by - 2, 2 * near_by))
        step(centre - near_by)
        ahead = reach + 1 + near_by
        if ahead < depth:
            forward(ahead)
        if sent < depth:
            share(sent, sent + 1)
            sent += 2
        step(centre + near_by)

    for r in range(rows):
        start = pl.multiple_of((r + reach) * block + q * piece, piece)
        for c in range(0, mids * 2):
            if 0 <= c - r < band:
                part[r * piece : (r + 1) * piece, c * block : (c + 1) * block] = cur[
                    pl.ds(start, piece), c * block : (c + 1) * block
                ]
            else:
                blank = jnp.zeros((piece, block), jnp.bfloat16)
                part[r * piece : (r + 1) * piece, c * block : (c + 1) * block] = blank
                part_square[r * piece : (r + 1) * piece, c * block : (c + 1) * block] = blank

    def columns_of(c, source):
        low, high = max(0, c - span), min(mids, c + span + 1)
        first, last = max(0, c - 2 * span), min(tiles, c + 1)
        product = jnp.dot(
            source[first * 2 * piece : last * 2 * piece, low * tile : high * tile],
            cur[low * tile : high * tile, c * tile : (c + 1) * tile],
            preferred_element_type=jnp.float32,
        )
        for r in range(2 * first, 2 * last):
            for b in range(2):
                w = 2 * c + b - r
                if 0 <= w < band:
                    at = (r - 2 * first) * piece
                    yield r, w, product[at : at + piece, b * block : (b + 1) * block]

    for c in range(mids):
        for r, w, value in columns_of(c, part):
            part_square[
                r * piece : (r + 1) * piece, (r + w) * block : (r + w + 1) * block
            ] = masked(value, r, w).astype(jnp.bfloat16)
    for c in range(mids):
        for r, w, value in columns_of(c, part_square):
            before = part[r * piece : (r + 1) * piece, (r + w) * block : (r + w + 1) * block]
            after = (3.0 * before.astype(jnp.float32) - value * scale) * 0.5
            o_ref[r, w] = masked(after, r, w).astype(jnp.bfloat16)

    for j in range(depth):
        for side in range(2):
            for stage in range(4):
                copies[stage, side, j].wait_send()
    for side in range(2):
        flag_copies[side].wait_send()


def per_device(layers, grids, band_blocks, retained):
    rows, band, block, _ = band_blocks.shape
    reach = (band - 1) // 2
    depth = 2 * reach
    piece = block // layers
    dtype = band_blocks.dtype
    anywhere = pl.BlockSpec(memory_space=pl.ANY)
    tile = 2 * block
    total = (rows + 2 * depth) * block
    middle = (rows + depth) * block
    return pl.pallas_call(
        functools.partial(purify, (layers, grids, rows, reach, block)),
        out_shape=jax.ShapeDtypeStruct((rows, band, piece, block), dtype),
        in_specs=[anywhere, anywhere],
        out_specs=pl.BlockSpec(memory_space=pltpu.VMEM),
        scratch_shapes=[
            pltpu.VMEM((rows, band, block, block), dtype),
            pltpu.VMEM((2, depth, reach + 1, block, block), dtype),
            pltpu.VMEM((2, rows, band), retained.dtype),
            pltpu.SMEM((3, rows, band), retained.dtype),
            pltpu.VMEM((total, total), dtype),
            pltpu.VMEM((middle, middle), dtype),
            pltpu.VMEM((tile, (reach + 1) * tile), dtype),
            pltpu.VMEM((rows * piece, middle), dtype),
            pltpu.VMEM((rows * piece, middle), dtype),
            pltpu.SemaphoreType.DMA((4, 2, depth)),
            pltpu.SemaphoreType.DMA((4, 2, depth)),
            pltpu.SemaphoreType.DMA((2,)),
            pltpu.SemaphoreType.DMA((2,)),
            pltpu.SemaphoreType.DMA((2,)),
        ],
        compiler_params=pltpu.CompilerParams(
            collective_id=0, has_side_effects=True, vmem_limit_bytes=60 * 1024 * 1024
        ),
        name="purify",
    )(band_blocks, retained)


def solution(mesh):
    return jax.shard_map(
        functools.partial(per_device, mesh.shape["layer"], mesh.shape["grid"]),
        mesh=mesh,
        in_specs=(P("grid", None, None, None), P("grid", None)),
        out_specs=P("grid", None, "layer", None),
        check_vma=False,
    )
```

time: 161 us -> 37.3 us (0.23)
  waiting for transfers between devices: 104 us -> 0 us
  Pallas kernels: 0 us -> 35.2 us
  matrix products: 23.9 us -> 0 us
  between operations: 13.6 us -> 0.01 us
  starting transfers between devices: 11 us -> 0 us
  other arithmetic: 3.59 us -> 0 us
  local copies, waits for them, and re-layouts: 4.62 us -> 2.03 us
    all_gather x2 -> x0, waiting for transfers between devices: 80.6 us -> none  [per_device(): halo_rows = lax.all_gather(halo_part, 'layer', axis=2, tiled=True)]
    pallas_call x0 -> x1, Pallas kernels: none -> 35.2 us  [per_device(): pl.pallas_call(functools.partial(purify, (layers, grids, rows, reach, blo...]
    dot_general x36 -> x0, matrix products: 23.9 us -> none  [strip_product(): jnp.einsum('rab,rwbc->rwac', left_rows[:, offset], source, preferred_elem...]
    ppermute x4 -> x0, waiting for transfers between devices: 23.6 us -> none  [the longest x2 19.2 us: extended(): lax.ppermute(lax.slice_in_dim(block, block.shape[dim] - width, None, axis...]
    ppermute x4 -> x0, starting transfers between devices: 10.9 us -> none  [the longest x2 6.36 us: extended(): lax.ppermute(lax.slice_in_dim(block, 0, width, axis=dim), axis, backward)]
    concatenate x2 -> x0, other arithmetic: 2.51 us -> none  [extended(): block = jnp.concatenate([low, block, high], axis=dim)]
    unnamed x18 -> x1, local copies, waits for them, and re-layouts: 3.52 us -> 2.03 us
  transfers between devices with their start and end apart: 6 -> 0, of which waited for: 6 -> 0; matrix products, arithmetic and copies ran while one was open for 0% -> 0% of each run, Pallas kernels for 0% -> 0%
where the time goes in v2:
time: 37.3 us; the launch traced here: 37.2 us
  Pallas kernels  35.2 us (94%)
  local copies, waits for them, and re-layouts  2.03 us (5%)
    pallas_call x1, Pallas kernels, per_device(): pl.pallas_call(functools.partial(purify, (layers, grids, rows, reach, blo...  35.2 us
    unnamed x1, local copies, waits for them, and re-layouts  2.03 us

profile of v2, /device:TPU:0, one launch (start us, length us, event | category | flops | bytes accessed | tf_op | source)
XLA Modules:
  0.0 37.2 jit_solution(6678145489443184438)
XLA Ops:
  0.0 35.2 %purify.1 = bf16[10,9,32,128]{3,2,1,0:T(8,128)(2,1)} custom-call(bf16[10,9,128,128]{3,2,1,0:T(8,128)(2,1)} %x_hbm.1, s32[10,9]{1,0:T(8,128)} %r_hbm.1), custom_call_target="tpu_custom_call" | custom-call | tf_op jit(solution)/shard_map/purify/pallas_call | solution.py:277
  35.2 2.0 %copy.4 = bf16[10,9,32,128]{3,2,1,0:T(8,128)(2,1)} copy(bf16[10,9,32,128]{3,2,1,0:T(8,128)(2,1)} %purify.1) | data formatting | bytes 1474560

commit v3 on v2

--- a/solution.py
+++ b/solution.py
@@ -75,14 +75,21 @@
             there = halo.at[side, j, 0:count, mine, :]
             beyond = halo.at[side, j, 0:count, fars, :]
             if side == 0:
-                source = x_hbm.at[rows - 1 - j, reach : reach + count, mine, :]
+                source = x_hbm.at[rows - 1 - j, reach : reach + count]
             else:
-                source = x_hbm.at[j, reach + 1 - count : reach + 1, mine, :]
-            copies[0, side, j] = copy(0, side, j, source, there, sides[side])
-            copies[1, side, j] = copy(1, side, j, there, there, (far, g))
+                source = x_hbm.at[j, reach + 1 - count : reach + 1]
+            copies[0, side, j] = copy(0, side, j, source.at[:, mine, :], there, sides[side])
+            if j < depth - 1:
+                copies[1, side, j] = copy(1, side, j, there, there, (far, g))
+            else:
+                copies[1, side, j] = copy(
+                    1, side, j, source.at[:, fars, :], beyond, sides[side]
+                )
             copies[2, side, j] = copy(2, side, j, there, there, (near, g))
             copies[3, side, j] = copy(3, side, j, beyond, beyond, (near, g))
             copies[0, side, j].start()
+            if j == depth - 1:
+                copies[1, side, j].start()
         if j == 1:
             for side in range(2):
                 flag_copies[side].start()
@@ -91,7 +98,8 @@
         for j in js:
             for side in range(2):
                 copies[0, side, j].wait_recv()
-                copies[1, side, j].start()
+                if j < depth - 1:
+                    copies[1, side, j].start()
                 copies[2, side, j].start()
 
     def share(*js):
@@ -130,9 +138,11 @@
         high = min(2 * span, d + span)
         return low, high + 1
 
-    def step(i):
+    every = range(2 * span + 1)
+
+    def squares(i, which):
         rows_at = slice((i + span) * tile, (i + span + 1) * tile)
-        for d in range(2 * span + 1):
+        for d in which:
             low, high = ranges(d)
             inner = slice((i + low) * tile, (i + high) * tile)
             columns = slice((i + d) * tile, (i + d + 1) * tile)
@@ -151,15 +161,18 @@
                     else:
                         value = jnp.zeros((block, block), jnp.bfloat16)
                     at = d * tile + b * block
-                    strip[a * block : (a + 1) * block, at : at + block] = value
-        for d in range(2 * span + 1):
+                    strip[i, a * block : (a + 1) * block, at : at + block] = value
+
+    def cubes(i):
+        rows_at = slice((i + span) * tile, (i + span + 1) * tile)
+        for d in every:
             if not 0 <= i + d - span < mids:
                 continue
             low, high = ranges(d)
             inner = slice((i + low) * tile, (i + high) * tile)
             columns = slice((i + d) * tile, (i + d + 1) * tile)
             product = jnp.dot(
-                strip[:, low * tile : high * tile],
+                strip[i, :, low * tile : high * tile],
                 wide[inner, columns],
                 preferred_element_type=jnp.float32,
             )
@@ -179,6 +192,15 @@
                     at = (i + d - span) * tile + b * block
                     cur[down : down + block, at : at + block] = result
 
+    def early(i):
+        if span <= i < span + tiles:
+            return [d for d in every if span <= i + d - span < span + tiles]
+        return [d for d in every if (d > span if i < centre else d < span)]
+
+    def rest(i):
+        squares(i, [d for d in every if d not in early(i)])
+        cubes(i)
+
     empty = jnp.zeros((block, block), jnp.bfloat16)
     for t in range(total // 2):
         r = 2 * t - depth
@@ -196,39 +218,18 @@
             if c < 0 or c >= rows:
                 put(c, r, value.T)
 
-    forward(*range(reach))
-    step(centre)
-    for side in range(2):
-        flag_copies[side].wait_recv()
-        landed = pltpu.make_async_copy(flags.at[side], r3.at[2 * side], local.at[0])
-        landed.start()
-        landed.wait()
-    forward(reach)
-    share(0, 1)
-    forward(reach + 1)
-    sent = 2
-    for near_by in range(1, span + tiles // 2 + 1):
-        build(*range(2 * near_by - 2, 2 * near_by))
-        step(centre - near_by)
-        ahead = reach + 1 + near_by
-        if ahead < depth:
-            forward(ahead)
-        if sent < depth:
-            share(sent, sent + 1)
-            sent += 2
-        step(centre + near_by)
-
-    for r in range(rows):
-        start = pl.multiple_of((r + reach) * block + q * piece, piece)
-        for c in range(0, mids * 2):
-            if 0 <= c - r < band:
-                part[r * piece : (r + 1) * piece, c * block : (c + 1) * block] = cur[
-                    pl.ds(start, piece), c * block : (c + 1) * block
-                ]
-            else:
-                blank = jnp.zeros((piece, block), jnp.bfloat16)
-                part[r * piece : (r + 1) * piece, c * block : (c + 1) * block] = blank
-                part_square[r * piece : (r + 1) * piece, c * block : (c + 1) * block] = blank
+    def gather():
+        for r in range(rows):
+            start = pl.multiple_of((r + reach) * block + q * piece, piece)
+            for c in range(0, mids * 2):
+                if 0 <= c - r < band:
+                    part[r * piece : (r + 1) * piece, c * block : (c + 1) * block] = cur[
+                        pl.ds(start, piece), c * block : (c + 1) * block
+                    ]
+                else:
+                    blank = jnp.zeros((piece, block), jnp.bfloat16)
+                    part[r * piece : (r + 1) * piece, c * block : (c + 1) * block] = blank
+                    part_square[r * piece : (r + 1) * piece, c * block : (c + 1) * block] = blank
 
     def columns_of(c, source):
         low, high = max(0, c - span), min(mids, c + span + 1)
@@ -245,11 +246,59 @@
                     at = (r - 2 * first) * piece
                     yield r, w, product[at : at + piece, b * block : (b + 1) * block]
 
-    for c in range(mids):
-        for r, w, value in columns_of(c, part):
-            part_square[
-                r * piece : (r + 1) * piece, (r + w) * block : (r + w + 1) * block
-            ] = masked(value, r, w).astype(jnp.bfloat16)
+    def part_squares(which):
+        for c in which:
+            for r, w, value in columns_of(c, part):
+                part_square[
+                    r * piece : (r + 1) * piece, (r + w) * block : (r + w + 1) * block
+                ] = masked(value, r, w).astype(jnp.bfloat16)
+
+    squares(centre, every)
+    cubes(centre)
+    forward(0, 1)
+    squares(centre - 1, early(centre - 1))
+    forward(2)
+    squares(centre + 1, early(centre + 1))
+    squares(centre - 2, early(centre - 2))
+    forward(3)
+    share(0, 1)
+    squares(centre + 2, early(centre + 2))
+    for side in range(2):
+        flag_copies[side].wait_recv()
+        landed = pltpu.make_async_copy(flags.at[side], r3.at[2 * side], local.at[0])
+        landed.start()
+        landed.wait()
+    build(0, 1)
+    rest(centre - 1)
+    forward(4)
+    share(2)
+    rest(centre + 1)
+    share(3)
+    forward(5)
+    build(2, 3)
+    rest(centre - 2)
+    forward(6)
+    share(4)
+    rest(centre + 2)
+    forward(7)
+    share(5)
+    squares(centre - 3, early(centre - 3))
+    squares(centre + 3, early(centre + 3))
+    gather()
+    share(7)
+    build(4, 5)
+    rest(centre - 3)
+    share(6)
+    rest(centre + 3)
+    squares(centre - 4, early(centre - 4))
+    squares(centre + 4, early(centre + 4))
+    inner_columns = range(centre - 1, centre + 2)
+    part_squares(inner_columns)
+    build(6, 7)
+    rest(centre - 4)
+    rest(centre + 4)
+    part_squares([c for c in range(mids) if c not in inner_columns])
+
     for c in range(mids):
         for r, w, value in columns_of(c, part_square):
             before = part[r * piece : (r + 1) * piece, (r + w) * block : (r + w + 1) * block]
@@ -286,7 +335,7 @@
             pltpu.SMEM((3, rows, band), retained.dtype),
             pltpu.VMEM((total, total), dtype),
             pltpu.VMEM((middle, middle), dtype),
-            pltpu.VMEM((tile, (reach + 1) * tile), dtype),
+            pltpu.VMEM((middle // tile, tile, (reach + 1) * tile), dtype),
             pltpu.VMEM((rows * piece, middle), dtype),
             pltpu.VMEM((rows * piece, middle), dtype),
             pltpu.SemaphoreType.DMA((4, 2, depth)),

time: 37.3 us -> 36.4 us (0.976)
  Pallas kernels: 35.2 us -> 34.2 us
    pallas_call x1, Pallas kernels: 35.2 us -> 34.2 us  [per_device(): pl.pallas_call(functools.partial(purify, (layers, grids, rows, reach, blo...]
where the time goes in v3:
time: 36.4 us; the launch traced here: 36.3 us
  Pallas kernels  34.2 us (94%)
  local copies, waits for them, and re-layouts  2.03 us (6%)
    pallas_call x1, Pallas kernels, per_device(): pl.pallas_call(functools.partial(purify, (layers, grids, rows, reach, blo...  34.2 us
    unnamed x1, local copies, waits for them, and re-layouts  2.03 us

profile of v3, /device:TPU:0, one launch (start us, length us, event | category | flops | bytes accessed | tf_op | source)
XLA Modules:
  0.0 36.3 jit_solution(8360998608958473173)
XLA Ops:
  0.0 34.2 %purify.1 = bf16[10,9,32,128]{3,2,1,0:T(8,128)(2,1)} custom-call(bf16[10,9,128,128]{3,2,1,0:T(8,128)(2,1)} %x_hbm.1, s32[10,9]{1,0:T(8,128)} %r_hbm.1), custom_call_target="tpu_custom_call" | custom-call | tf_op jit(solution)/shard_map/purify/pallas_call | solution.py:326
  34.2 2.0 %copy.4 = bf16[10,9,32,128]{3,2,1,0:T(8,128)(2,1)} copy(bf16[10,9,32,128]{3,2,1,0:T(8,128)(2,1)} %purify.1) | data formatting | bytes 1474560

commit v4 on v3

--- a/solution.py
+++ b/solution.py
@@ -79,17 +79,10 @@
             else:
                 source = x_hbm.at[j, reach + 1 - count : reach + 1]
             copies[0, side, j] = copy(0, side, j, source.at[:, mine, :], there, sides[side])
-            if j < depth - 1:
-                copies[1, side, j] = copy(1, side, j, there, there, (far, g))
-            else:
-                copies[1, side, j] = copy(
-                    1, side, j, source.at[:, fars, :], beyond, sides[side]
-                )
+            copies[1, side, j] = copy(1, side, j, there, there, (far, g))
             copies[2, side, j] = copy(2, side, j, there, there, (near, g))
             copies[3, side, j] = copy(3, side, j, beyond, beyond, (near, g))
             copies[0, side, j].start()
-            if j == depth - 1:
-                copies[1, side, j].start()
         if j == 1:
             for side in range(2):
                 flag_copies[side].start()
@@ -98,8 +91,7 @@
         for j in js:
             for side in range(2):
                 copies[0, side, j].wait_recv()
-                if j < depth - 1:
-                    copies[1, side, j].start()
+                copies[1, side, j].start()
                 copies[2, side, j].start()
 
     def share(*js):
@@ -285,11 +277,11 @@
     squares(centre - 3, early(centre - 3))
     squares(centre + 3, early(centre + 3))
     gather()
-    share(7)
     build(4, 5)
     rest(centre - 3)
     share(6)
     rest(centre + 3)
+    share(7)
     squares(centre - 4, early(centre - 4))
     squares(centre + 4, early(centre + 4))
     inner_columns = range(centre - 1, centre + 2)

time: 36.4 us -> 35.9 us (0.986)
  Pallas kernels: 34.2 us -> 33.7 us
    pallas_call x1, Pallas kernels: 34.2 us -> 33.7 us  [per_device(): pl.pallas_call(functools.partial(purify, (layers, grids, rows, reach, blo...]
where the time goes in v4:
time: 35.9 us; the launch traced here: 35.8 us
  Pallas kernels  33.7 us (94%)
  local copies, waits for them, and re-layouts  2.03 us (6%)
    pallas_call x1, Pallas kernels, per_device(): pl.pallas_call(functools.partial(purify, (layers, grids, rows, reach, blo...  33.7 us
    unnamed x1, local copies, waits for them, and re-layouts  2.03 us

profile of v4, /device:TPU:0, one launch (start us, length us, event | category | flops | bytes accessed | tf_op | source)
XLA Modules:
  0.0 35.8 jit_solution(11875231810531226627)
XLA Ops:
  0.0 33.7 %purify.1 = bf16[10,9,32,128]{3,2,1,0:T(8,128)(2,1)} custom-call(bf16[10,9,128,128]{3,2,1,0:T(8,128)(2,1)} %x_hbm.1, s32[10,9]{1,0:T(8,128)} %r_hbm.1), custom_call_target="tpu_custom_call" | custom-call | tf_op jit(solution)/shard_map/purify/pallas_call | solution.py:318
  33.7 2.0 %copy.4 = bf16[10,9,32,128]{3,2,1,0:T(8,128)(2,1)} copy(bf16[10,9,32,128]{3,2,1,0:T(8,128)(2,1)} %purify.1) | data formatting | bytes 1474560
